TPU v7x, 256 devices: a whole 4x4x8 slice. The times are simulated.
256 devices in a mesh: dp: 16 (over x, y_hi, core), fsdp: 16 (over y_lo, z).
Axes of the slice: x: 4, y: 4 (y_hi: 2, y_lo: 2; y = y_hi * 2 + y_lo), z: 8, core: 2. Of those that a mesh axis runs over, the one named last changes fastest.
Arguments:
- tokens: bfloat16 [8192, 2048], P('dp'), may hold values from -6 to 6
- expert_ids: int32 [8192, 2], P('dp'), may hold values from 0 to 7, as said below
- route_probs: float32 [8192, 2], P('dp'), may hold values from 0.1 to 1
- gate_w: bfloat16 [2, 2048, 7168], P(None, 'dp', 'fsdp'), may hold values from -0.125 to 0.125
- up_w: bfloat16 [2, 2048, 7168], P(None, 'dp', 'fsdp'), may hold values from -0.125 to 0.125
- down_w: bfloat16 [2, 7168, 2048], P(None, 'fsdp', 'dp'), may hold values from -0.0625 to 0.0625
- out_grad: bfloat16 [8192, 2048], P('dp'), may hold values from -6 to 6
Outputs:
- mixed: bfloat16 [8192, 2048], P('dp')
- token_grad: bfloat16 [8192, 2048], P('dp')
- gate_grad: bfloat16 [2, 2048, 7168], P(None, 'dp', 'fsdp')
- up_grad: bfloat16 [2, 2048, 7168], P(None, 'dp', 'fsdp')
- down_grad: bfloat16 [2, 7168, 2048], P(None, 'fsdp', 'dp')
Inputs may be any that keep to these rules, and one draw needn't show every extreme that they name: `expert_ids`: the two entries of a row differ. In each aligned block of 512 rows (the rows of one index of dp) every expert is named by at most 256 rows, and one of experts 0 to 1 by exactly 256 rows.
All inputs are finite; a program needn't handle non-finite values.
Results may differ from a plain program's by a relative error of at most 0.018.
Values may be sent and summed in bfloat16 or wider, within the bound.
A program may use at most 128 MiB of HBM per device.

v0:
```python
import jax
import jax.numpy as jnp
from jax import lax
from jax.sharding import PartitionSpec as P


def slot_layout(expert_ids, route_probs, expert, slot_cap):
    token_count = expert_ids.shape[0]
    matches = expert_ids == expert
    chosen = jnp.any(matches, axis=1)
    weight_token = jnp.sum(jnp.where(matches, route_probs, jnp.float32(0.0)), axis=1)
    position = jnp.cumsum(chosen.astype(jnp.int32)) - 1
    slot_index = lax.broadcasted_iota(jnp.int32, (slot_cap, token_count), 0)
    token_index = lax.broadcasted_iota(jnp.int32, (slot_cap, token_count), 1)
    matched_slots = (position[None, :] == slot_index) & chosen[None, :]
    slot_token = jnp.sum(jnp.where(matched_slots, token_index, 0), axis=1)
    slot_valid = jnp.any(matched_slots, axis=1)
    slot_weight = jnp.where(slot_valid, jnp.take(weight_token, slot_token), jnp.float32(0.0))
    token_slot = jnp.clip(position, 0, slot_cap - 1)
    return (chosen, token_slot, slot_token, slot_valid, slot_weight)


def group_total(partial_value):
    return lax.psum(partial_value.astype(jnp.bfloat16), "fsdp")


def body(tokens, expert_ids, route_probs, gate_w, up_w, down_w, out_grad):
    token_count = tokens.shape[0]
    width = tokens.shape[1]
    slot_cap = token_count // 2
    window = gate_w.shape[0]
    mixed_part = jnp.zeros((token_count, width), jnp.float32)
    stored = []
    for expert in range(window):
        chosen, token_slot, slot_token, slot_valid, slot_weight = slot_layout(
            expert_ids, route_probs, expert, slot_cap
        )
        gate_full, up_full, down_full = (
            lax.all_gather(gate_w[expert], "dp", axis=0, tiled=True),
            lax.all_gather(up_w[expert], "dp", axis=0, tiled=True),
            lax.all_gather(down_w[expert], "dp", axis=1, tiled=True),
        )
        slot_input = jnp.take(tokens, slot_token, axis=0) * slot_valid[:, None].astype(tokens.dtype)
        gate_act = jnp.dot(slot_input, gate_full, preferred_element_type=jnp.float32)
        up_act = jnp.dot(slot_input, up_full, preferred_element_type=jnp.float32)
        hidden = (jax.nn.silu(gate_act) * up_act).astype(jnp.bfloat16)
        expert_out = (
            jnp.dot(hidden, down_full, preferred_element_type=jnp.float32) * slot_weight[:, None]
        )
        mixed_part = mixed_part + jnp.where(
            chosen[:, None], jnp.take(expert_out, token_slot, axis=0), jnp.float32(0.0)
        )
        stored.append(
            (
                chosen,
                token_slot,
                slot_token,
                slot_weight,
                slot_input,
                gate_act,
                up_act,
                hidden,
                gate_full,
                up_full,
                down_full,
            )
        )
    mixed = group_total(mixed_part)
    grad_part = jnp.zeros((token_count, width), jnp.float32)
    gate_grads, up_grads, down_grads = ([], [], [])
    for expert in range(window):
        (
            chosen,
            token_slot,
            slot_token,
            slot_weight,
            slot_input,
            gate_act,
            up_act,
            hidden,
            gate_full,
            up_full,
            down_full,
        ) = stored[expert]
        slot_grad = (
            jnp.take(out_grad, slot_token, axis=0).astype(jnp.float32) * slot_weight[:, None]
        ).astype(jnp.bfloat16)
        down_term = lax.dot_general(
            hidden, slot_grad, (((0,), (0,)), ((), ())), preferred_element_type=jnp.float32
        )
        hidden_grad = lax.dot_general(
            slot_grad, down_full, (((1,), (1,)), ((), ())), preferred_element_type=jnp.float32
        )
        sigma = jax.nn.sigmoid(gate_act)
        up_act_grad = (hidden_grad * gate_act * sigma).astype(jnp.bfloat16)
        gate_act_grad = (hidden_grad * up_act * sigma * (1.0 + gate_act * (1.0 - sigma))).astype(
            jnp.bfloat16
        )
        gate_term = lax.dot_general(
            slot_input, gate_act_grad, (((0,), (0,)), ((), ())), preferred_element_type=jnp.float32
        )
        up_term = lax.dot_general(
            slot_input, up_act_grad, (((0,), (0,)), ((), ())), preferred_element_type=jnp.float32
        )
        input_grad = lax.dot_general(
            gate_act_grad, gate_full, (((1,), (1,)), ((), ())), preferred_element_type=jnp.float32
        )
        input_grad = input_grad + lax.dot_general(
            up_act_grad, up_full, (((1,), (1,)), ((), ())), preferred_element_type=jnp.float32
        )
        grad_part = grad_part + jnp.where(
            chosen[:, None], jnp.take(input_grad, token_slot, axis=0), jnp.float32(0.0)
        )
        gate_sum, up_sum, down_sum = (
            lax.psum_scatter(
                gate_term.astype(jnp.bfloat16), "dp", scatter_dimension=0, tiled=True
            ).astype(jnp.float32),
            lax.psum_scatter(
                up_term.astype(jnp.bfloat16), "dp", scatter_dimension=0, tiled=True
            ).astype(jnp.float32),
            lax.psum_scatter(
                down_term.astype(jnp.bfloat16), "dp", scatter_dimension=1, tiled=True
            ).astype(jnp.float32),
        )
        gate_grads.append(gate_sum.astype(jnp.bfloat16))
        up_grads.append(up_sum.astype(jnp.bfloat16))
        down_grads.append(down_sum.astype(jnp.bfloat16))
    gate_grad = jnp.stack(gate_grads)
    up_grad = jnp.stack(up_grads)
    down_grad = jnp.stack(down_grads)
    token_grad = group_total(grad_part)
    return (mixed, token_grad, gate_grad, up_grad, down_grad)


def solution(mesh):
    placed = (
        P("dp", None),
        P("dp", None),
        P("dp", None),
        P(None, "dp", "fsdp"),
        P(None, "dp", "fsdp"),
        P(None, "fsdp", "dp"),
        P("dp", None),
    )
    return jax.shard_map(
        body,
        mesh=mesh,
        in_specs=placed,
        out_specs=(
            P("dp", None),
            P("dp", None),
            P(None, "dp", "fsdp"),
            P(None, "dp", "fsdp"),
            P(None, "fsdp", "dp"),
        ),
        check_vma=False,
    )
```

profile of v0, /device:TPU:4, one launch (start us, length us, event | category | flops | bytes accessed | tf_op | source)
XLA Modules:
  0.0 1003.4 jit_solution(5504983384310768062)
XLA Ops:
  7.2 1.8 fusion.32
  9.1 1.7 fusion.31
  10.8 1.7 fusion.30
  16.1 1.9 gather_fusion.4
  18.1 1.4 gather_fusion.3
  19.5 5.2 gather_fusion.8
  24.7 41.6 %all-gather.21.cloned.1.call-done = bf16[1,2048,448]{1,2,0:T(8,128)(2,1)} async-done(((bf16[1,128,448]{1,2,0:T(8,128)(2,1)}), bf16[1,2048,448]{1,2,0:T(8,128)(2,1)}) %all-gather.21.cloned.1.call-update) | async-done | bytes 1835024 | tf_op jit(solution)/shard_map/all_gather | solution.py:40
  66.2 3.1 fusion.8
  69.3 52.5 %all-gather.19.cloned.1.call-done = bf16[1,2048,448]{1,2,0:T(8,128)(2,1)} async-done(((bf16[1,128,448]{1,2,0:T(8,128)(2,1)}), bf16[1,2048,448]{1,2,0:T(8,128)(2,1)}) %all-gather.19.cloned.1.call-update) | async-done | bytes 1835024 | tf_op jit(solution)/shard_map/all_gather | solution.py:39
  121.8 3.0 fusion.12
  124.9 52.0 %all-gather.23.cloned.1.call-done = bf16[1,448,2048]{2,1,0:T(8,128)(2,1)} async-done(((bf16[1,448,128]{2,1,0:T(8,128)(2,1)}), bf16[1,448,2048]{2,1,0:T(8,128)(2,1)}) %all-gather.23.cloned.1.call-update) | async-done | bytes 1835024 | tf_op jit(solution)/shard_map/all_gather | solution.py:41
  176.9 3.7 multiply_convert_fusion.2
  180.5 0.7 copy-done.10
  181.2 2.0 convolution_convert_fusion.4
  183.2 3.8 copy.22
  187.3 2.3 gather_fusion
  189.6 4.3 gather_fusion.6
  194.1 1.9 gather_fusion.1
  196.1 36.2 %all-gather.15.cloned.1.call-done = bf16[1,2048,448]{1,2,0:T(8,128)(2,1)} async-done(((bf16[1,128,448]{1,2,0:T(8,128)(2,1)}), bf16[1,2048,448]{1,2,0:T(8,128)(2,1)}) %all-gather.15.cloned.1.call-update) | async-done | bytes 1835024 | tf_op jit(solution)/shard_map/all_gather | solution.py:40
  232.3 3.0 fusion.18
  235.4 52.4 %all-gather.13.cloned.1.call-done = bf16[1,2048,448]{1,2,0:T(8,128)(2,1)} async-done(((bf16[1,128,448]{1,2,0:T(8,128)(2,1)}), bf16[1,2048,448]{1,2,0:T(8,128)(2,1)}) %all-gather.13.cloned.1.call-update) | async-done | bytes 1835024 | tf_op jit(solution)/shard_map/all_gather | solution.py:39
  287.8 3.1 fusion.22
  290.9 51.8 %all-gather.17.cloned.1.call-done = bf16[1,448,2048]{2,1,0:T(8,128)(2,1)} async-done(((bf16[1,448,128]{2,1,0:T(8,128)(2,1)}), bf16[1,448,2048]{2,1,0:T(8,128)(2,1)}) %all-gather.17.cloned.1.call-update) | async-done | bytes 1835024 | tf_op jit(solution)/shard_map/all_gather | solution.py:41
  342.7 3.3 multiply_convert_fusion.4
  346.0 0.7 copy-done.16
  346.7 2.0 convolution_convert_fusion.5
  348.7 2.4 copy.20
  351.2 2.0 convolution_convert_fusion.1
  353.2 2.5 copy.16
  355.8 2.0 convolution_convert_fusion.3
  357.8 2.4 copy.12
  360.3 0.8 convolution_convert_fusion
  361.1 2.5 copy.18
  363.7 0.8 convolution_convert_fusion.2
  364.5 2.4 copy.14
  367.2 2.3 convolution_multiply_fusion.1
  369.5 3.6 gather_fusion.2
  373.1 2.4 fusion.20
  375.5 0.7 convolution_add_fusion.1
  376.3 3.6 gather_fusion.7
  379.9 2.2 convolution_multiply_fusion
  382.2 3.6 gather_fusion.5
  385.8 2.4 fusion.10
  388.1 0.7 convolution_add_fusion
  388.9 3.6 gather_fusion.9
  392.4 9.4 fusion.1
  401.9 22.4 %reduce-scatter.29.cloned.1.call-done = bf16[128,448]{1,0:T(8,128)(2,1)} async-done(((bf16[2048,448]{1,0:T(8,128)(2,1)}), bf16[128,448]{1,0:T(8,128)(2,1)}) %reduce-scatter.29.cloned.1.call-update) | async-done | bytes 114704
  424.3 1.0 copy.23
  425.3 80.9 %reduce-scatter.27.cloned.1.call-done = bf16[128,448]{1,0:T(8,128)(2,1)} async-done(((bf16[2048,448]{1,0:T(8,128)(2,1)}), bf16[128,448]{1,0:T(8,128)(2,1)}) %reduce-scatter.27.cloned.1.call-update) | async-done | bytes 114704
  506.3 1.0 copy.21
  507.3 80.9 %reduce-scatter.23.cloned.1.call-done = bf16[128,448]{1,0:T(8,128)(2,1)} async-done(((bf16[2048,448]{1,0:T(8,128)(2,1)}), bf16[128,448]{1,0:T(8,128)(2,1)}) %reduce-scatter.23.cloned.1.call-update) | async-done | bytes 114704
  588.3 1.0 copy.17
  589.3 80.8 %reduce-scatter.19.cloned.1.call-done = bf16[128,448]{1,0:T(8,128)(2,1)} async-done(((bf16[2048,448]{1,0:T(8,128)(2,1)}), bf16[128,448]{1,0:T(8,128)(2,1)}) %reduce-scatter.19.cloned.1.call-update) | async-done | bytes 114704
  670.1 1.0 copy.13
  671.1 81.0 %reduce-scatter.25.cloned.1.call-done = bf16[128,448]{1,0:T(8,128)(2,1)} async-done(((bf16[2048,448]{1,0:T(8,128)(2,1)}), bf16[128,448]{1,0:T(8,128)(2,1)}) %reduce-scatter.25.cloned.1.call-update) | async-done | bytes 114704
  752.1 1.0 copy.19
  753.1 80.8 %reduce-scatter.21.cloned.1.call-done = bf16[128,448]{1,0:T(8,128)(2,1)} async-done(((bf16[2048,448]{1,0:T(8,128)(2,1)}), bf16[128,448]{1,0:T(8,128)(2,1)}) %reduce-scatter.21.cloned.1.call-update) | async-done | bytes 114704
  833.9 1.0 copy.15
  835.0 0.7 pad_maximum_fusion.2
  835.7 0.7 pad_maximum_fusion.1
  836.4 0.7 pad_maximum_fusion
  837.1 155.1 %all-reduce.3.cloned.1.call-done = (bf16[512,2048]{1,0:T(8,128)(2,1)}, bf16[512,2048]{1,0:T(8,128)(2,1)}) async-done(((bf16[512,2048]{1,0:T(8,128)(2,1)}, bf16[512,2048]{1,0:T(8,128)(2,1)}), (bf16[512,2048]{1,0:T(8,128)(2,1)}, bf16[512,2048]{1,0:T(8,128)(2,1)})) %all-reduce.3.cloned.1.call-update) | async-done | bytes 4194320 | tf_op jit(solution)/shard_map/psum | solution.py:24
  992.2 3.3 copy.26
  995.5 1.3 copy.27
  (93 shorter events, 4.7 us)
Async XLA Ops:
  7.2 10.9 %copy-start = (bf16[512,2048]{1,0:T(8,128)(2,1)S(1)}, bf16[512,2048]{1,0:T(8,128)(2,1)}, u32[]{:S(2)}) copy-start(bf16[512,2048]{1,0:T(8,128)(2,1)} %param.13) | copy-start | bytes 6291460
  7.2 7.1 copy-start.18
  7.2 8.9 copy-start.19
  7.2 59.0 %all-gather.21.cloned.1.call-start = ((), (), s32[]{:S(2)}) async-start(), calls=%async_computation.10 | async-start | bytes 1949696 | tf_op jit(solution)/shard_map/all_gather | solution.py:40
  9.1 112.8 %all-gather.19.cloned.1.call-start = ((), (), s32[]{:S(2)}) async-start(), calls=%async_computation.9 | async-start | bytes 1949696 | tf_op jit(solution)/shard_map/all_gather | solution.py:39
  10.8 166.1 %all-gather.23.cloned.1.call-start = ((), (), s32[]{:S(2)}) async-start(), calls=%async_computation.11 | async-start | bytes 1949696 | tf_op jit(solution)/shard_map/all_gather | solution.py:41
  12.5 219.8 %all-gather.15.cloned.1.call-start = ((), (), s32[]{:S(2)}) async-start(), calls=%async_computation.7 | async-start | bytes 1949696 | tf_op jit(solution)/shard_map/all_gather | solution.py:40
  13.1 274.7 %all-gather.13.cloned.1.call-start = ((), (), s32[]{:S(2)}) async-start(), calls=%async_computation.6 | async-start | bytes 1949696 | tf_op jit(solution)/shard_map/all_gather | solution.py:39
  13.7 329.0 %all-gather.17.cloned.1.call-start = ((), (), s32[]{:S(2)}) async-start(), calls=%async_computation.8 | async-start | bytes 1949696 | tf_op jit(solution)/shard_map/all_gather | solution.py:41
  14.3 410.0 %reduce-scatter.29.cloned.1.call-start = ((), (), s32[]{:S(2)}) async-start(), calls=%async_computation.17 | async-start | bytes 2228224
  176.9 4.3 copy-start.7
  180.5 0.7 copy-start.10
  187.0 319.3 %reduce-scatter.27.cloned.1.call-start = ((), (), s32[]{:S(2)}) async-start(), calls=%async_computation.16 | async-start | bytes 2228224
  189.6 42.7 %copy-start.5 = (bf16[256,2048]{1,0:T(8,128)(2,1)S(1)}, bf16[256,2048]{1,0:T(8,128)(2,1)}, u32[]{:S(2)}) copy-start(bf16[256,2048]{1,0:T(8,128)(2,1)} %gather_fusion) | copy-start | bytes 3145732
  193.9 148.7 %copy-start.6 = (bf16[256,2048]{1,0:T(8,128)(2,1)}, bf16[256,2048]{1,0:T(8,128)(2,1)S(1)}, u32[]{:S(2)}) copy-start(bf16[256,2048]{1,0:T(8,128)(2,1)S(1)} %gather_fusion.6) | copy-start | bytes 3145732
  346.0 0.7 copy-start.16
  348.7 2.5 copy-start.12
  351.2 237.1 %reduce-scatter.23.cloned.1.call-start = ((), (), s32[]{:S(2)}) async-start(), calls=%async_computation.14 | async-start | bytes 2228224
  353.2 2.6 copy-start.14
  355.8 314.3 %reduce-scatter.19.cloned.1.call-start = ((), (), s32[]{:S(2)}) async-start(), calls=%async_computation.12 | async-start | bytes 2228224
  360.2 391.8 %reduce-scatter.25.cloned.1.call-start = ((), (), s32[]{:S(2)}) async-start(), calls=%async_computation.15 | async-start | bytes 2228224
  361.1 2.7 copy-start.8
  363.6 470.3 %reduce-scatter.21.cloned.1.call-start = ((), (), s32[]{:S(2)}) async-start(), calls=%async_computation.13 | async-start | bytes 2228224
  364.5 2.7 copy-start.17
  366.9 625.3 %all-reduce.3.cloned.1.call-start = ((), (), s32[]{:S(2)}) async-start(), calls=%async_computation.18 | async-start | bytes 8388608 | tf_op jit(solution)/shard_map/psum | solution.py:24
  369.5 3.6 copy-start.15
  373.1 2.4 copy-start.4
  373.1 2.4 copy-start.13
  376.3 3.6 copy-start.11
  382.1 3.6 copy-start.9
  385.8 2.4 copy-start.3
  992.2 3.3 copy-start.2
  992.2 4.6 copy-start.1
Sparse Core Ops, SparseCore 0:
  11.2 55.0 all-gather.20
  69.3 52.4 all-gather.18
  124.4 52.4 all-gather.22
  179.8 52.4 all-gather.14
  235.3 52.4 all-gather.12
  290.2 52.4 all-gather.16
  346.9 77.3 reduce-scatter.28
  428.5 77.7 reduce-scatter.26
  510.5 77.6 reduce-scatter.22
  592.3 77.7 reduce-scatter.18
  674.3 77.7 reduce-scatter.24
  756.2 77.7 reduce-scatter.20
  837.2 154.9 all-reduce.2
where the time goes:
time: 1000 us
  waiting for transfers between devices  870 us (87%)
  local copies, waits for them, and re-layouts  65.4 us (7%)
  matrix products  39.4 us (4%)
  between operations  14.3 us (1%)
  other arithmetic  13.1 us (1%)
    unnamed x19, waiting for transfers between devices  429 us
    psum x1, waiting for transfers between devices, group_total(): return lax.psum(partial_value.astype(jnp.bfloat16), 'fsdp')  155 us
    all_gather x2, waiting for transfers between devices, body(): lax.all_gather(gate_w[expert], 'dp', axis=0, tiled=True)  105 us
    all_gather x2, waiting for transfers between devices, body(): lax.all_gather(down_w[expert], 'dp', axis=1, tiled=True)  104 us
    all_gather x2, waiting for transfers between devices, body(): lax.all_gather(up_w[expert], 'dp', axis=0, tiled=True)  77.8 us
    unnamed x54, local copies, waits for them, and re-layouts  28.4 us
  transfers between devices with their start and end apart: 13, of which 13 were waited for; matrix products, arithmetic and copies ran while one was open for 11% of the time, Pallas kernels for 0%

commit v1 on v0

--- a/solution.py
+++ b/solution.py
@@ -2,6 +2,11 @@
 import jax.numpy as jnp
 from jax import lax
 from jax.sharding import PartitionSpec as P
+
+
+def gather_over(value, axis, dim):
+    sent = jnp.stack([value] * lax.axis_size(axis))
+    return jnp.concatenate(lax.all_to_all(sent, axis, 0, 0), axis=dim)
 
 
 def slot_layout(expert_ids, route_probs, expert, slot_cap):
@@ -37,7 +42,7 @@
         )
         gate_full, up_full, down_full = (
             lax.all_gather(gate_w[expert], "dp", axis=0, tiled=True),
-            lax.all_gather(up_w[expert], "dp", axis=0, tiled=True),
+            gather_over(up_w[expert], "dp", 0),
             lax.all_gather(down_w[expert], "dp", axis=1, tiled=True),
         )
         slot_input = jnp.take(tokens, slot_token, axis=0) * slot_valid[:, None].astype(tokens.dtype)

time: 1000 us -> 922 us (0.922)
  waiting for transfers between devices: 870 us -> 771 us
  starting transfers between devices: 0.93 us -> 15.3 us
    all_gather x2 -> x0, waiting for transfers between devices: 77.8 us -> none  [body(): lax.all_gather(up_w[expert], 'dp', axis=0, tiled=True)]
    all_gather x2, waiting for transfers between devices: 105 us -> 67.6 us  [body(): lax.all_gather(gate_w[expert], 'dp', axis=0, tiled=True)]
    all_to_all x0 -> x2, waiting for transfers between devices: none -> 14.9 us  [gather_over(): return jnp.concatenate(lax.all_to_all(sent, axis, 0, 0), axis=dim)]
    all_to_all x0 -> x2, starting transfers between devices: none -> 14.4 us  [gather_over(): return jnp.concatenate(lax.all_to_all(sent, axis, 0, 0), axis=dim)]
    unnamed x19 -> x17, waiting for transfers between devices: 429 us -> 428 us
    unnamed x54 -> x52, local copies, waits for them, and re-layouts: 28.4 us -> 28.4 us
  transfers between devices with their start and end apart: 13 -> 13, of which waited for: 13 -> 12; matrix products, arithmetic and copies ran while one was open for 11% -> 12% of each run, Pallas kernels for 0% -> 0%
where the time goes in v1:
time: 922 us; the launch traced here: 921 us
  waiting for transfers between devices  771 us (84%)
  local copies, waits for them, and re-layouts  67.8 us (7%)
  matrix products  39.8 us (4%)
  starting transfers between devices  15.3 us (2%)
  between operations  14.3 us (2%)
  other arithmetic  13.1 us (1%)
    unnamed x17, waiting for transfers between devices  428 us
    psum x1, waiting for transfers between devices, group_total(): return lax.psum(partial_value.astype(jnp.bfloat16), 'fsdp')  155 us
    all_gather x2, waiting for transfers between devices, body(): lax.all_gather(down_w[expert], 'dp', axis=1, tiled=True)  105 us
    all_gather x2, waiting for transfers between devices, body(): lax.all_gather(gate_w[expert], 'dp', axis=0, tiled=True)  67.6 us
    unnamed x52, local copies, waits for them, and re-layouts  28.4 us
  transfers between devices with their start and end apart: 13, of which 12 were waited for; matrix products, arithmetic and copies ran while one was open for 12% of the time, Pallas kernels for 0%

profile of v1, /device:TPU:4, one launch (start us, length us, event | category | flops | bytes accessed | tf_op | source)
XLA Modules:
  0.0 921.0 jit_solution(7571448398140306365)
XLA Ops:
  7.2 1.8 fusion.35
  9.1 1.7 fusion.34
  11.5 1.0 slice_bitcast_fusion.1
  12.5 1.6 stack.33
  14.1 7.6 all-to-all-start
  24.0 1.9 gather_fusion.1
  26.0 1.4 gather_fusion
  27.4 5.2 gather_fusion.6
  32.6 14.9 %all-to-all-done = bf16[16,128,448]{1,2,0:T(8,128)(2,1)} async-done(((bf16[16,128,448]{1,2,0:T(8,128)(2,1)}), bf16[16,128,448]{1,2,0:T(8,128)(2,1)}, u32[]{:S(2)}, u32[]{:S(2)}) %all-to-all-start) | async-done | bytes 1835040 | tf_op jit(solution)/shard_map/all_to_all | solution.py:9
  47.4 1.6 stack.34
  49.0 6.9 all-to-all-start.1
  55.9 3.0 fusion.8
  59.0 34.3 %all-gather.9.cloned.1.call-done = bf16[1,2048,448]{1,2,0:T(8,128)(2,1)} async-done(((bf16[1,128,448]{1,2,0:T(8,128)(2,1)}), bf16[1,2048,448]{1,2,0:T(8,128)(2,1)}) %all-gather.9.cloned.1.call-update) | async-done | bytes 1835024 | tf_op jit(solution)/shard_map/all_gather | solution.py:44
  93.3 3.1 fusion.22
  96.4 53.5 %all-gather.11.cloned.1.call-done = bf16[1,448,2048]{2,1,0:T(8,128)(2,1)} async-done(((bf16[1,448,128]{2,1,0:T(8,128)(2,1)}), bf16[1,448,2048]{2,1,0:T(8,128)(2,1)}) %all-gather.11.cloned.1.call-update) | async-done | bytes 1835024 | tf_op jit(solution)/shard_map/all_gather | solution.py:46
  149.8 3.7 multiply_convert_fusion.4
  154.2 2.0 convolution_convert_fusion.5
  156.2 3.8 copy.28
  160.3 2.3 gather_fusion.3
  162.6 4.3 gather_fusion.8
  167.1 1.9 gather_fusion.4
  169.1 3.1 fusion.5
  172.2 33.3 %all-gather.13.cloned.1.call-done = bf16[1,2048,448]{1,2,0:T(8,128)(2,1)} async-done(((bf16[1,128,448]{1,2,0:T(8,128)(2,1)}), bf16[1,2048,448]{1,2,0:T(8,128)(2,1)}) %all-gather.13.cloned.1.call-update) | async-done | bytes 1835024 | tf_op jit(solution)/shard_map/all_gather | solution.py:44
  205.5 3.0 fusion.15
  208.5 51.8 %all-gather.15.cloned.1.call-done = bf16[1,448,2048]{2,1,0:T(8,128)(2,1)} async-done(((bf16[1,448,128]{2,1,0:T(8,128)(2,1)}), bf16[1,448,2048]{2,1,0:T(8,128)(2,1)}) %all-gather.15.cloned.1.call-update) | async-done | bytes 1835024 | tf_op jit(solution)/shard_map/all_gather | solution.py:46
  260.3 3.3 multiply_convert_fusion.2
  264.3 2.0 convolution_convert_fusion.4
  266.4 2.4 copy.30
  268.9 0.8 convolution_convert_fusion.1
  269.7 2.5 copy.24
  272.2 0.8 convolution_convert_fusion.3
  273.0 2.4 copy.20
  275.5 0.7 convolution_convert_fusion
  276.3 2.5 copy.26
  278.9 0.7 convolution_convert_fusion.2
  279.7 2.4 copy.22
  282.4 2.3 convolution_multiply_fusion
  284.7 3.6 gather_fusion.5
  288.3 2.3 fusion.13
  290.6 2.2 convolution_add_fusion
  292.9 3.6 gather_fusion.9
  296.5 2.2 convolution_multiply_fusion.1
  298.7 3.6 gather_fusion.2
  302.3 2.3 fusion.20
  304.6 2.2 convolution_add_fusion.1
  306.9 3.6 gather_fusion.7
  310.5 9.4 %fusion.1 = (bf16[512,2048]{1,0:T(8,128)(2,1)}, bf16[512,2048]{1,0:T(8,128)(2,1)}) fusion(f32[512,2048]{1,0:T(8,128)} %gather_fusion.9, f32[512,2048]{1,0:T(8,128)} %gather_fusion.7, pred[512]{0:T(512)(128)(4,1)S(1)} %get-tuple-element.16, pred[512]{0:T(512)(128)(4,1)S(1)} %get-tuple-element.14, pred[512]{0:T(512)(128)(4,1)S(1)} %get-tuple-element.11, ...), kind=kLoop, calls=%fused_computation.12 | loop fusion | flops 12582912 | bytes 20973568 | tf_op jit(solution)/shard_map/convert_element_type | solution.py:29
  319.9 21.9 %reduce-scatter.27.cloned.1.call-done = bf16[128,448]{1,0:T(8,128)(2,1)} async-done(((bf16[2048,448]{1,0:T(8,128)(2,1)}), bf16[128,448]{1,0:T(8,128)(2,1)}) %reduce-scatter.27.cloned.1.call-update) | async-done | bytes 114704
  341.8 1.0 copy.29
  342.8 80.8 %reduce-scatter.29.cloned.1.call-done = bf16[128,448]{1,0:T(8,128)(2,1)} async-done(((bf16[2048,448]{1,0:T(8,128)(2,1)}), bf16[128,448]{1,0:T(8,128)(2,1)}) %reduce-scatter.29.cloned.1.call-update) | async-done | bytes 114704
  423.6 1.0 copy.31
  424.7 80.9 %reduce-scatter.23.cloned.1.call-done = bf16[128,448]{1,0:T(8,128)(2,1)} async-done(((bf16[2048,448]{1,0:T(8,128)(2,1)}), bf16[128,448]{1,0:T(8,128)(2,1)}) %reduce-scatter.23.cloned.1.call-update) | async-done | bytes 114704
  505.6 1.0 copy.25
  506.7 80.9 %reduce-scatter.19.cloned.1.call-done = bf16[128,448]{1,0:T(8,128)(2,1)} async-done(((bf16[2048,448]{1,0:T(8,128)(2,1)}), bf16[128,448]{1,0:T(8,128)(2,1)}) %reduce-scatter.19.cloned.1.call-update) | async-done | bytes 114704
  587.6 1.0 copy.21
  588.6 80.9 %reduce-scatter.25.cloned.1.call-done = bf16[128,448]{1,0:T(8,128)(2,1)} async-done(((bf16[2048,448]{1,0:T(8,128)(2,1)}), bf16[128,448]{1,0:T(8,128)(2,1)}) %reduce-scatter.25.cloned.1.call-update) | async-done | bytes 114704
  669.6 1.0 copy.27
  670.6 80.8 %reduce-scatter.21.cloned.1.call-done = bf16[128,448]{1,0:T(8,128)(2,1)} async-done(((bf16[2048,448]{1,0:T(8,128)(2,1)}), bf16[128,448]{1,0:T(8,128)(2,1)}) %reduce-scatter.21.cloned.1.call-update) | async-done | bytes 114704
  751.4 1.0 copy.23
  752.5 0.7 pad_maximum_fusion.2
  753.2 0.7 pad_maximum_fusion.1
  754.6 155.2 %all-reduce.3.cloned.1.call-done = (bf16[512,2048]{1,0:T(8,128)(2,1)}, bf16[512,2048]{1,0:T(8,128)(2,1)}) async-done(((bf16[512,2048]{1,0:T(8,128)(2,1)}, bf16[512,2048]{1,0:T(8,128)(2,1)}), (bf16[512,2048]{1,0:T(8,128)(2,1)}, bf16[512,2048]{1,0:T(8,128)(2,1)})) %all-reduce.3.cloned.1.call-update) | async-done | bytes 4194320 | tf_op jit(solution)/shard_map/psum | solution.py:29
  909.8 3.3 copy.52
  913.1 1.3 copy.53
  (91 shorter events, 6.3 us)
Async XLA Ops:
  7.2 18.8 %copy-start = (bf16[512,2048]{1,0:T(8,128)(2,1)S(1)}, bf16[512,2048]{1,0:T(8,128)(2,1)}, u32[]{:S(2)}) copy-start(bf16[512,2048]{1,0:T(8,128)(2,1)} %param.13) | copy-start | bytes 6291460
  7.2 86.1 %all-gather.9.cloned.1.call-start = ((), (), s32[]{:S(2)}) async-start(), calls=%async_computation.8 | async-start | bytes 1949696 | tf_op jit(solution)/shard_map/all_gather | solution.py:44
  9.0 140.8 %all-gather.11.cloned.1.call-start = ((), (), s32[]{:S(2)}) async-start(), calls=%async_computation.9 | async-start | bytes 1949696 | tf_op jit(solution)/shard_map/all_gather | solution.py:46
  10.8 194.7 %all-gather.13.cloned.1.call-start = ((), (), s32[]{:S(2)}) async-start(), calls=%async_computation.10 | async-start | bytes 1949696 | tf_op jit(solution)/shard_map/all_gather | solution.py:44
  14.1 8.2 copy-start.17
  14.1 9.9 %copy-start.18 = (f32[512,2]{0,1:T(2,128)S(1)}, f32[512,2]{0,1:T(2,128)}, u32[]{:S(2)}) copy-start(f32[512,2]{0,1:T(2,128)} %param.15) | copy-start | bytes 12292
  14.1 33.4 %all-to-all-start = ((bf16[16,128,448]{1,2,0:T(8,128)(2,1)}), bf16[16,128,448]{1,2,0:T(8,128)(2,1)}, u32[]{:S(2)}, u32[]{:S(2)}) async-start(bf16[16,128,448]{1,2,0:T(8,128)(2,1)} %stack.33), calls=%async_computation | async-start | bytes 3670016 | tf_op jit(solution)/shard_map/all_to_all | solution.py:9
  21.7 238.7 %all-gather.15.cloned.1.call-start = ((), (), s32[]{:S(2)}) async-start(), calls=%async_computation.11 | async-start | bytes 1949696 | tf_op jit(solution)/shard_map/all_gather | solution.py:46
  49.0 120.1 %all-to-all-start.1 = ((bf16[16,128,448]{1,2,0:T(8,128)(2,1)}), bf16[16,128,448]{1,2,0:T(8,128)(2,1)}, u32[]{:S(2)}, u32[]{:S(2)}) async-start(bf16[16,128,448]{1,2,0:T(8,128)(2,1)} %stack.34), calls=%async_computation.1 | async-start | bytes 3670016 | tf_op jit(solution)/shard_map/all_to_all | solution.py:9
  55.9 285.9 %reduce-scatter.27.cloned.1.call-start = ((), (), s32[]{:S(2)}) async-start(), calls=%async_computation.16 | async-start | bytes 2228224
  149.8 4.3 copy-start.5
  153.5 0.7 copy-start.9
  160.0 263.6 %reduce-scatter.29.cloned.1.call-start = ((), (), s32[]{:S(2)}) async-start(), calls=%async_computation.17 | async-start | bytes 2228224
  162.6 6.5 copy-start.3
  166.9 93.4 %copy-start.6 = (bf16[256,2048]{1,0:T(8,128)(2,1)}, bf16[256,2048]{1,0:T(8,128)(2,1)S(1)}, u32[]{:S(2)}) copy-start(bf16[256,2048]{1,0:T(8,128)(2,1)S(1)} %gather_fusion.8) | copy-start | bytes 3145732
  263.7 0.7 copy-start.15
  268.8 236.8 %reduce-scatter.23.cloned.1.call-start = ((), (), s32[]{:S(2)}) async-start(), calls=%async_computation.14 | async-start | bytes 2228224
  269.6 2.6 copy-start.7
  272.2 315.4 %reduce-scatter.19.cloned.1.call-start = ((), (), s32[]{:S(2)}) async-start(), calls=%async_computation.12 | async-start | bytes 2228224
  273.0 2.5 copy-start.4
  273.0 2.5 copy-start.11
  275.5 394.1 %reduce-scatter.25.cloned.1.call-start = ((), (), s32[]{:S(2)}) async-start(), calls=%async_computation.15 | async-start | bytes 2228224
  276.3 2.6 copy-start.13
  278.8 472.6 %reduce-scatter.21.cloned.1.call-start = ((), (), s32[]{:S(2)}) async-start(), calls=%async_computation.13 | async-start | bytes 2228224
  279.7 2.7 copy-start.16
  282.1 627.7 %all-reduce.3.cloned.1.call-start = ((), (), s32[]{:S(2)}) async-start(), calls=%async_computation.18 | async-start | bytes 8388608 | tf_op jit(solution)/shard_map/psum | solution.py:29
  284.7 3.6 copy-start.14
  288.3 2.3 copy-start.12
  292.9 3.6 copy-start.10
  298.7 3.6 copy-start.8
  909.8 3.3 copy-start.2
  909.8 4.6 copy-start.1
Sparse Core Ops, SparseCore 0:
  11.1 82.1 all-gather.8
  96.4 53.3 all-gather.10
  153.0 52.4 all-gather.12
  207.9 52.4 all-gather.14
  264.4 77.3 reduce-scatter.26
  345.9 77.7 reduce-scatter.28
  427.9 77.7 reduce-scatter.22
  509.9 77.7 reduce-scatter.18
  591.8 77.6 reduce-scatter.24
  673.6 77.7 reduce-scatter.20
  754.7 155.0 all-reduce.2
